TPU v7x, 32 devices: a whole 2x2x4 slice. The times are simulated.
32 devices in a mesh: dp: 16 (over z, y, core), tp: 2 (over x).
Axes of the slice: x: 2, y: 2, z: 4, core: 2. Of those that a mesh axis runs over, the one named last changes fastest.
Arguments:
- tokens: bfloat16 [16384, 768], P(('dp', 'tp')), may hold values from -6 to 6
- segment_ids: int32 [16384], P('dp'), may hold values from 0 to 63, never falling along the last dimension, each value on 1 to 512 neighbouring positions
- first_gain: float32 [768], replicated, may hold values from 0.5 to 1.5
- first_shift: float32 [768], replicated, may hold values from -1.75 to 1.75
- qkv_weight: bfloat16 [768, 3, 768], P(None, None, 'tp'), may hold values from -0.21875 to 0.21875
- query_bias: float32 [768], P('tp'), may hold values from -3 to 3
- value_bias: float32 [768], P('tp'), may hold values from -3 to 3
- out_weight: bfloat16 [768, 768], P('tp'), may hold values from -0.875 to 0.875
- out_bias: float32 [768], replicated, may hold values from -1.75 to 1.75
- second_gain: float32 [768], replicated, may hold values from 0.5 to 1.5
- second_shift: float32 [768], replicated, may hold values from -1.75 to 1.75
- up_weight: bfloat16 [768, 3072], P(None, 'tp'), may hold values from -0.21875 to 0.21875
- up_bias: float32 [3072], P('tp'), may hold values from -3 to 3
- down_weight: bfloat16 [3072, 768], P('tp'), may hold values from -0.109375 to 0.109375
- down_bias: float32 [768], replicated, may hold values from -1.75 to 1.75
- grad_out: bfloat16 [16384, 768], P(('dp', 'tp')), may hold values from -6 to 6
Outputs:
- layer_out: bfloat16 [16384, 768], P(('dp', 'tp'))
- tokens_grad: bfloat16 [16384, 768], P(('dp', 'tp'))
- first_gain_grad: float32 [768], replicated
- first_shift_grad: float32 [768], replicated
- qkv_grad: float32 [768, 3, 768], P(None, None, 'tp')
- query_bias_grad: float32 [768], P('tp')
- value_bias_grad: float32 [768], P('tp')
- out_weight_grad: float32 [768, 768], P('tp')
- out_bias_grad: float32 [768], replicated
- second_gain_grad: float32 [768], replicated
- second_shift_grad: float32 [768], replicated
- up_weight_grad: float32 [768, 3072], P(None, 'tp')
- up_bias_grad: float32 [3072], P('tp')
- down_weight_grad: float32 [3072, 768], P('tp')
- down_bias_grad: float32 [768], replicated
Inputs may be any that keep to these rules, and one draw needn't show every extreme that they name: `segment_ids`: segment numbers never fall along the patches; each segment holds 1 to 512 patches, one exactly 512.
All inputs are finite; a program needn't handle non-finite values.
Results may differ from a plain program's by a relative error of at most 0.018.
Values may be sent and summed in bfloat16 or wider, within the bound.
No kernel may reach another device: no remote copies, remote signals or barrier semaphores. Data moves between devices by JAX's collectives and lax.ppermute only.
A program may use at most 192 MiB of HBM per device.

v0:
```python
import jax
import jax.numpy as jnp
from jax import lax
from jax.sharding import PartitionSpec as P

HEAD = 64


EPS = 1e-06
MASKED = -1e30


def normalize(values, gain, shift):
    center = values - jnp.mean(values, axis=-1, keepdims=True)
    spread = jnp.mean(center * center, axis=-1, keepdims=True)
    return center * lax.rsqrt(spread + EPS) * gain + shift


def gelu_exact(values):
    return jax.nn.gelu(values, approximate=False)


def on_device(
    tokens,
    segment_ids,
    first_gain,
    first_shift,
    qkv_weight,
    query_bias,
    value_bias,
    out_weight,
    out_bias,
    second_gain,
    second_shift,
    up_weight,
    up_bias,
    down_weight,
    down_bias,
    grad_out,
):
    f32 = jnp.float32
    bf16 = jnp.bfloat16
    width = tokens.shape[1]
    local_width = qkv_weight.shape[2]
    heads_here = local_width // HEAD
    row_count = segment_ids.shape[0]
    block = min(512, row_count)
    blocks = row_count // block
    factor = HEAD ** (-0.5)
    qkv_flat = qkv_weight.reshape(width, 3 * local_width)
    tokens_f = tokens.astype(f32)
    first_normed, first_pull = jax.vjp(normalize, tokens_f, first_gain, first_shift)
    gathered = lax.all_gather(first_normed.astype(bf16), "tp", axis=0, tiled=True)
    projected = jnp.dot(gathered, qkv_flat, preferred_element_type=f32).reshape(
        row_count, 3, local_width
    )
    queries = (projected[:, 0] + query_bias).astype(bf16).reshape(row_count, heads_here, HEAD)
    keys_all = projected[:, 1].astype(bf16).reshape(row_count, heads_here, HEAD)
    values_all = (projected[:, 2] + value_bias).astype(bf16).reshape(row_count, heads_here, HEAD)
    same_doc = segment_ids[:, None] == segment_ids[None, :]

    def block_scores(index):
        query_blk = queries[index * block : (index + 1) * block]
        raw = jnp.einsum("qhd,khd->hqk", query_blk, keys_all, preferred_element_type=f32) * factor
        return (
            jnp.where(same_doc[index * block : (index + 1) * block][None], raw, MASKED),
            query_blk,
        )

    mixed_list = []
    log_totals = []
    for index in range(blocks):
        scores, query_blk = block_scores(index)
        peak = jnp.max(scores, axis=-1, keepdims=True)
        expon = jnp.exp(scores - peak)
        denom = jnp.sum(expon, axis=-1, keepdims=True)
        weights_low = (expon / denom).astype(bf16)
        mixed = jnp.einsum("hqk,khd->qhd", weights_low, values_all, preferred_element_type=f32)
        mixed_list.append(mixed.astype(bf16).reshape(block, local_width))
        log_totals.append(peak + jnp.log(denom))
    attended = jnp.concatenate(mixed_list, axis=0)
    middle = (
        tokens_f
        + lax.psum_scatter(
            jnp.dot(attended, out_weight, preferred_element_type=f32).astype(jnp.bfloat16),
            "tp",
            scatter_dimension=0,
            tiled=True,
        ).astype(jnp.float32)
        + out_bias
    )
    second_normed, second_pull = jax.vjp(normalize, middle, second_gain, second_shift)
    gathered_two = lax.all_gather(second_normed.astype(bf16), "tp", axis=0, tiled=True)
    pre_act = jnp.dot(gathered_two, up_weight, preferred_element_type=f32) + up_bias
    hidden_f, gelu_pull = jax.vjp(gelu_exact, pre_act)
    hidden = hidden_f.astype(bf16)
    result = (
        middle
        + lax.psum_scatter(
            jnp.dot(hidden, down_weight, preferred_element_type=f32).astype(jnp.bfloat16),
            "tp",
            scatter_dimension=0,
            tiled=True,
        ).astype(jnp.float32)
        + down_bias
    )
    layer_out = result.astype(bf16)
    grad_f = grad_out.astype(f32)
    grad_rows = lax.all_gather(grad_out, "tp", axis=0, tiled=True)
    down_grad = jnp.einsum("tf,td->fd", hidden, grad_rows, preferred_element_type=f32)
    hidden_grad = jnp.einsum("td,fd->tf", grad_rows, down_weight, preferred_element_type=f32)
    pre_grad = gelu_pull(hidden_grad)[0]
    up_bias_grad = jnp.sum(pre_grad, axis=0)
    pre_low = pre_grad.astype(bf16)
    up_grad = jnp.einsum("td,tf->df", gathered_two, pre_low, preferred_element_type=f32)
    second_back = lax.psum_scatter(
        jnp.einsum("tf,df->td", pre_low, up_weight, preferred_element_type=f32).astype(
            jnp.bfloat16
        ),
        "tp",
        scatter_dimension=0,
        tiled=True,
    ).astype(jnp.float32)
    middle_back, second_gain_part, second_shift_part = second_pull(second_back)
    middle_grad = grad_f + middle_back
    out_bias_part = jnp.sum(middle_grad, axis=0)
    down_bias_part = jnp.sum(grad_f, axis=0)
    middle_low = middle_grad.astype(bf16)
    grad_attn_rows = lax.all_gather(middle_low, "tp", axis=0, tiled=True)
    out_grad = jnp.einsum("tc,td->cd", attended, grad_attn_rows, preferred_element_type=f32)
    attended_grad = (
        jnp.einsum("td,cd->tc", grad_attn_rows, out_weight, preferred_element_type=f32)
        .astype(bf16)
        .reshape(row_count, heads_here, HEAD)
    )
    query_parts = []
    key_grad = jnp.zeros((row_count, heads_here, HEAD), f32)
    value_grad = jnp.zeros((row_count, heads_here, HEAD), f32)
    for index in range(blocks):
        scores, query_blk = block_scores(index)
        weights_f = jnp.exp(scores - log_totals[index])
        weights_low = weights_f.astype(bf16)
        grad_blk = attended_grad[index * block : (index + 1) * block]
        value_grad = value_grad + jnp.einsum(
            "hqk,qhd->khd", weights_low, grad_blk, preferred_element_type=f32
        )
        weight_grad = jnp.einsum("qhd,khd->hqk", grad_blk, values_all, preferred_element_type=f32)
        inner = jnp.sum(weights_f * weight_grad, axis=-1, keepdims=True)
        score_low = (weights_f * (weight_grad - inner)).astype(bf16)
        query_parts.append(
            jnp.einsum("hqk,khd->qhd", score_low, keys_all, preferred_element_type=f32) * factor
        )
        key_grad = (
            key_grad
            + jnp.einsum("hqk,qhd->khd", score_low, query_blk, preferred_element_type=f32) * factor
        )
    query_grad = jnp.concatenate(query_parts, axis=0).reshape(row_count, local_width)
    key_grad = key_grad.reshape(row_count, local_width)
    value_grad = value_grad.reshape(row_count, local_width)
    query_bias_grad = jnp.sum(query_grad, axis=0)
    value_bias_grad = jnp.sum(value_grad, axis=0)
    proj_grad = (
        jnp.stack([query_grad, key_grad, value_grad], axis=1)
        .astype(bf16)
        .reshape(row_count, 3 * local_width)
    )
    qkv_grad = jnp.einsum("td,tc->dc", gathered, proj_grad, preferred_element_type=f32).reshape(
        width, 3, local_width
    )
    first_back = lax.psum_scatter(
        jnp.einsum("tc,dc->td", proj_grad, qkv_flat, preferred_element_type=f32).astype(
            jnp.bfloat16
        ),
        "tp",
        scatter_dimension=0,
        tiled=True,
    ).astype(jnp.float32)
    tokens_back, first_gain_part, first_shift_part = first_pull(first_back)
    tokens_grad = (middle_grad + tokens_back).astype(bf16)
    (
        first_gain_grad,
        first_shift_grad,
        out_bias_grad,
        second_gain_grad,
        second_shift_grad,
        down_bias_grad,
    ) = lax.psum(
        (
            first_gain_part,
            first_shift_part,
            out_bias_part,
            second_gain_part,
            second_shift_part,
            down_bias_part,
        ),
        ("dp", "tp"),
    )
    qkv_grad, query_bias_grad, value_bias_grad, out_grad, up_grad, up_bias_grad, down_grad = (
        lax.psum(
            (
                qkv_grad,
                query_bias_grad,
                value_bias_grad,
                out_grad,
                up_grad,
                up_bias_grad,
                down_grad,
            ),
            "dp",
        )
    )
    return (
        layer_out,
        tokens_grad,
        first_gain_grad,
        first_shift_grad,
        qkv_grad,
        query_bias_grad,
        value_bias_grad,
        out_grad,
        out_bias_grad,
        second_gain_grad,
        second_shift_grad,
        up_grad,
        up_bias_grad,
        down_grad,
        down_bias_grad,
    )


def solution(mesh):
    in_specs = (
        P(("dp", "tp"), None),
        P("dp"),
        P(),
        P(),
        P(None, None, "tp"),
        P("tp"),
        P("tp"),
        P("tp", None),
        P(),
        P(),
        P(),
        P(None, "tp"),
        P("tp"),
        P("tp", None),
        P(),
        P(("dp", "tp"), None),
    )
    out_specs = (
        P(("dp", "tp"), None),
        P(("dp", "tp"), None),
        P(),
        P(),
        P(None, None, "tp"),
        P("tp"),
        P("tp"),
        P("tp", None),
        P(),
        P(),
        P(),
        P(None, "tp"),
        P("tp"),
        P("tp", None),
        P(),
    )
    return jax.shard_map(
        on_device, mesh=mesh, in_specs=in_specs, out_specs=out_specs, check_vma=False
    )
```

profile of v0, /device:TPU:0, one launch (start us, length us, event | category | flops | bytes accessed | tf_op | source)
XLA Modules:
  0.0 661.1 jit_solution(14338699882518699674)
XLA Ops:
  18.4 24.4 %all-gather.5.cloned.1.call-done = bf16[1024,768]{1,0:T(8,128)(2,1)} async-done(((bf16[512,768]{1,0:T(8,128)(2,1)}), bf16[1024,768]{1,0:T(8,128)(2,1)}) %all-gather.5.cloned.1.call-update) | async-done | bytes 1572880 | tf_op jit(solution)/shard_map/all_gather | solution.py:53
  72.3 26.0 %reduce-scatter.5.cloned.1.call-done = bf16[512,768]{1,0:T(8,128)(2,1)} async-done(((bf16[1024,768]{1,0:T(8,128)(2,1)}), bf16[512,768]{1,0:T(8,128)(2,1)}) %reduce-scatter.5.cloned.1.call-update) | async-done | bytes 786448 | tf_op jit(solution)/shard_map/reduce_scatter | solution.py:84
  104.7 26.7 %all-gather.7.cloned.1.call-done = bf16[1024,768]{1,0:T(8,128)(2,1)} async-done(((bf16[512,768]{1,0:T(8,128)(2,1)}), bf16[1024,768]{1,0:T(8,128)(2,1)}) %all-gather.7.cloned.1.call-update) | async-done | bytes 1572880 | tf_op jit(solution)/shard_map/all_gather | solution.py:93
  131.4 7.5 %fusion.71 = f32[1024,1536]{1,0:T(8,128)} fusion(bf16[1024,768]{1,0:T(8,128)(2,1)} %all-gather.7.cloned.1.call-done, bf16[768,1536]{1,0:T(8,128)(2,1)} %param.27), kind=kOutput, calls=%fused_computation.132 | convolution fusion | flops 2415919104 | bytes 10223616 | tf_op jit(solution)/shard_map/dot_general | solution.py:94
  138.8 21.2 %all-gather.9.cloned.1.call-done = bf16[1024,768]{1,0:T(8,128)(2,1)} async-done(((bf16[512,768]{1,0:T(8,128)(2,1)}), bf16[1024,768]{1,0:T(8,128)(2,1)}) %all-gather.9.cloned.1.call-update) | async-done | bytes 1572880 | tf_op jit(solution)/shard_map/all_gather | solution.py:109
  160.0 20.0 %fusion.61 = (f32[1536]{0:T(1024)}, bf16[1024,1536]{1,0:T(8,128)(2,1)S(1)}, f32[1024,1536]{1,0:T(8,128)}) fusion(f32[1024,1536]{1,0:T(8,128)} %fusion.71, f32[1536]{0:T(1024)} %param.28, bf16[1024,768]{1,0:T(8,128)(2,1)} %all-gather.9.cloned.1.call-done, bf16[1536,768]{1,0:T(8,128)(2,1)S(1)} %copy-done), kind=kOutput, calls=%fused_computation.123 | convolution fusion | flops 2532309504 | bytes 19673088 | tf_op jit(solution)/shard_map/td,fd->tf/dot_general | solution.py:111
  185.4 6.2 multiply_convert_fusion.2
  197.0 9.4 %all-gather.11.cloned.1.call-start = ((), (), s32[]{:S(2)}) async-start(), calls=%async_computation.10 | async-start | bytes 2359296 | tf_op jit(solution)/shard_map/all_gather | solution.py:129
  206.4 5.3 reduce-scatter.9.cloned.1.call-done
  217.8 22.2 %reduce-scatter.7.cloned.1.call-done = bf16[512,768]{1,0:T(8,128)(2,1)} async-done(((bf16[1024,768]{1,0:T(8,128)(2,1)}), bf16[512,768]{1,0:T(8,128)(2,1)}) %reduce-scatter.7.cloned.1.call-update) | async-done | bytes 786448 | tf_op jit(solution)/shard_map/reduce_scatter | solution.py:99
  247.2 25.2 %all-gather.11.cloned.1.call-done = bf16[1024,768]{1,0:T(8,128)(2,1)} async-done(((bf16[512,768]{1,0:T(8,128)(2,1)}), bf16[1024,768]{1,0:T(8,128)(2,1)}) %all-gather.11.cloned.1.call-update) | async-done | bytes 1572880 | tf_op jit(solution)/shard_map/all_gather | solution.py:129
  275.6 11.7 %multiply_reduce_fusion.1 = (f32[6,512]{1,0:T(8,128)S(1)}, f32[6,512,1024]{2,1,0:T(8,128)}) fusion(f32[6,512,1024]{2,1,0:T(8,128)} %copy-done.2, f32[6,512]{1,0:T(8,128)S(1)} %log_add_fusion.1, bf16[512,6,64]{0,2,1:T(8,128)(2,1)S(1)} %bitcast.108, bf16[1024,6,64]{0,2,1:T(8,128)(2,1)S(1)} %copy-done.12), kind=kOutput, calls=%fused_computation.4 | convolution fusion | flops 412087296 | bytes 26370048 | tf_op jit(solution)/shard_map/qhd,khd->hqk/dot_general | solution.py:147
  287.9 10.0 %multiply_convert_fusion.1 = bf16[6,512,1024]{2,1,0:T(8,128)(2,1)} fusion(f32[6,512,1024]{2,1,0:T(8,128)} %get-tuple-element.54, f32[6,512,1024]{2,1,0:T(8,128)S(1)} %bitcast.91, f32[6,512]{1,0:T(8,128)S(1)} %get-tuple-element.53, f32[6,512]{1,0:T(8,128)S(1)} %log_add_fusion.1), kind=kLoop, calls=%fused_computation.3 | loop fusion | flops 12582912 | bytes 31481856 | tf_op jit(solution)/shard_map/convert_element_type | solution.py:149
  297.9 6.3 fusion.69
  304.2 5.2 fusion.72
  312.8 7.6 %multiply_reduce_fusion = (f32[6,512]{1,0:T(8,128)S(1)}, f32[6,512,1024]{2,1,0:T(8,128)}) fusion(f32[6,512,1024]{2,1,0:T(8,128)S(1)} %bitcast.93, f32[6,512]{1,0:T(8,128)S(1)} %copy-done.31, bf16[512,6,64]{0,2,1:T(8,128)(2,1)} %bitcast.110, bf16[1024,6,64]{0,2,1:T(8,128)(2,1)} %copy-done.11), kind=kOutput, calls=%fused_computation.1 | convolution fusion | flops 412087296 | bytes 26370048 | tf_op jit(solution)/shard_map/qhd,khd->hqk/dot_general | solution.py:147
  320.4 4.9 bitcast_reduce_fusion
  327.6 9.5 %multiply_convert_fusion = bf16[6,512,1024]{2,1,0:T(8,128)(2,1)S(1)} fusion(f32[6,512,1024]{2,1,0:T(8,128)} %get-tuple-element.56, f32[6,512,1024]{2,1,0:T(8,128)} %copy-done.3, f32[6,512]{1,0:T(8,128)S(1)} %get-tuple-element.55, f32[6,512]{1,0:T(8,128)S(1)} %copy-done.31), kind=kLoop, calls=%fused_computation | loop fusion | flops 12582912 | bytes 31481856 | tf_op jit(solution)/shard_map/convert_element_type | solution.py:149
  353.5 7.4 %fusion.73 = f32[1536,768]{1,0:T(8,128)} fusion(bf16[1024,1536]{1,0:T(8,128)(2,1)} %copy-done.19, bf16[1024,768]{1,0:T(8,128)(2,1)} %all-gather.9.cloned.1.call-done), kind=kOutput, calls=%fused_computation.134 | convolution fusion | flops 2415919104 | bytes 9437184 | tf_op jit(solution)/shard_map/tf,td->fd/dot_general | solution.py:110
  360.9 4.3 fusion.42
  365.2 4.3 copy.39
  377.8 64.1 %all-reduce.1 = (f32[384]{0:T(512)}, f32[384]{0:T(512)}, f32[1536]{0:T(1024)}) all-reduce(f32[384]{0:T(512)S(1)} %reduce_sum.252, f32[384]{0:T(512)S(1)} %reduce_sum.254, f32[1536]{0:T(1024)S(1)} %copy-done.56), channel_id=1, replica_groups=mesh['dp'=16,'tp'=2] {'dp'}, use_global_device_ids=true, to_apply=%region_25.26 | all-reduce | flops 2304 | bytes 18432 | tf_op jit(solution)/shard_map/psum | solution.py:199
  445.9 39.0 %all-reduce = (f32[768]{0:T(1024)}, f32[768]{0:T(1024)}, f32[768]{0:T(1024)}, f32[768]{0:T(1024)}, f32[768]{0:T(1024)}, /*index=5*/f32[768]{0:T(1024)}) all-reduce(f32[768]{0:T(1024)S(1)} %get-tuple-element.17, f32[768]{0:T(1024)S(1)} %get-tuple-element.21, f32[768]{0:T(1024)S(1)} %copy-done.54, ...), channel_id=1, replica_groups=mesh['dp'=16,'tp'=2] {'dp','tp'}, use_global_device_ids=true, to_apply=%region_19.20 | all-reduce | flops 4608 | bytes 36864 | tf_op jit(solution)/shard_map/psum | solution.py:187
  486.4 156.9 %all-reduce.5.cloned.1.call-done = (f32[768,3,384]{2,0,1:T(8,128)}, f32[384,768]{1,0:T(8,128)}, f32[768,1536]{1,0:T(8,128)}, f32[1536,768]{1,0:T(8,128)}) async-done(((f32[768,3,384]{2,0,1:T(8,128)}, f32[384,768]{1,0:T(8,128)}, f32[768,1536]{1,0:T(8,128)}, f32[1536,768]{1,0:T(8,128)}), (f32[768,3,384]{2,0,1:T(8,128)}, f32[384,768]{1,0:T(8,128)}, f32[768,1536]{1,0:T(8,128)}, ...) | async-done | bytes 14155792 | tf_op jit(solution)/shard_map/psum | solution.py:199
  (236 shorter events, 120.8 us)
Async XLA Ops:
  7.2 152.8 %copy-start = (bf16[1536,768]{1,0:T(8,128)(2,1)S(1)}, bf16[1536,768]{1,0:T(8,128)(2,1)}, u32[]{:S(2)}) copy-start(bf16[1536,768]{1,0:T(8,128)(2,1)} %param.29) | copy-start | bytes 7077892
  7.2 35.5 %all-gather.5.cloned.1.call-start = ((), (), s32[]{:S(2)}) async-start(), calls=%async_computation.4 | async-start | bytes 2359296 | tf_op jit(solution)/shard_map/all_gather | solution.py:53
  12.7 85.6 %reduce-scatter.5.cloned.1.call-start = ((), (), s32[]{:S(2)}) async-start(), calls=%async_computation.5 | async-start | bytes 2359296 | tf_op jit(solution)/shard_map/reduce_scatter | solution.py:84
  69.0 29.2 %copy-start.4 = (bf16[512,768]{1,0:T(8,128)(2,1)S(1)}, bf16[512,768]{1,0:T(8,128)(2,1)}, u32[]{:S(2)}) copy-start(bf16[512,768]{1,0:T(8,128)(2,1)} %param.16) | copy-start | bytes 2359300
  69.0 29.2 %copy-start.32 = (f32[768]{0:T(1024)S(1)}, f32[768]{0:T(1024)}, u32[]{:S(2)}) copy-start(f32[768]{0:T(1024)} %param.24) | copy-start | bytes 9220
  71.9 30.0 %copy-start.41 = (f32[768]{0:T(1024)S(1)}, f32[768]{0:T(1024)}, u32[]{:S(2)}) copy-start(f32[768]{0:T(1024)} %param.25) | copy-start | bytes 9220
  72.0 59.4 %all-gather.7.cloned.1.call-start = ((), (), s32[]{:S(2)}) async-start(), calls=%async_computation.6 | async-start | bytes 2359296 | tf_op jit(solution)/shard_map/all_gather | solution.py:93
  104.0 56.0 %all-gather.9.cloned.1.call-start = ((), (), s32[]{:S(2)}) async-start(), calls=%async_computation.8 | async-start | bytes 2359296 | tf_op jit(solution)/shard_map/all_gather | solution.py:109
  104.6 107.1 %reduce-scatter.9.cloned.1.call-start = ((), (), s32[]{:S(2)}) async-start(), calls=%async_computation.9 | async-start | bytes 2359296 | tf_op jit(solution)/shard_map/reduce_scatter | solution.py:116
  160.0 21.6 %copy-start.59 = (bf16[768,1536]{1,0:T(8,128)(2,1)S(1)}, bf16[768,1536]{1,0:T(8,128)(2,1)}, u32[]{:S(2)}) copy-start(bf16[768,1536]{1,0:T(8,128)(2,1)} %param.27) | copy-start | bytes 7077892
  185.4 54.6 %reduce-scatter.7.cloned.1.call-start = ((), (), s32[]{:S(2)}) async-start(), calls=%async_computation.7 | async-start | bytes 2359296 | tf_op jit(solution)/shard_map/reduce_scatter | solution.py:99
  197.0 75.4 %all-gather.11.cloned.1.call-start = ((), (), s32[]{:S(2)}) async-start(), calls=%async_computation.10 | async-start | bytes 2359296 | tf_op jit(solution)/shard_map/all_gather | solution.py:129
  245.0 30.5 %copy-start.12 = (bf16[1024,6,64]{0,2,1:T(8,128)(2,1)S(1)}, bf16[1024,6,64]{0,2,1:T(8,128)(2,1)}, u32[]{:S(2)}) copy-start(bf16[1024,6,64]{0,2,1:T(8,128)(2,1)} %copy-done.11) | copy-start | bytes 2359300
  245.1 196.9 %reduce-scatter.11.cloned.1.call-start = ((), (), s32[]{:S(2)}) async-start(), calls=%async_computation.11 | async-start | bytes 2359296 | tf_op jit(solution)/shard_map/reduce_scatter | solution.py:170
  353.4 289.8 %all-reduce.5.cloned.1.call-start = ((), (), s32[]{:S(2)}) async-start(), calls=%async_computation.12 | async-start | bytes 28311552 | tf_op jit(solution)/shard_map/psum | solution.py:199
  377.0 65.0 %copy-start.37 = (f32[512]{0:T(512)S(1)}, f32[512]{0:T(512)}, u32[]{:S(2)}) copy-start(f32[512]{0:T(512)} %copy-done.36) | copy-start | bytes 6148
  377.0 65.0 %copy-start.38 = (f32[768]{0:T(1024)S(1)}, f32[768]{0:T(1024)}, u32[]{:S(2)}) copy-start(f32[768]{0:T(1024)} %param.18) | copy-start | bytes 9220
  377.0 66.8 %copy-start.46 = (f32[512]{0:T(512)S(1)}, f32[512]{0:T(512)}, u32[]{:S(2)}) copy-start(f32[512]{0:T(512)} %copy-done.45) | copy-start | bytes 6148
  377.0 66.8 %copy-start.43 = (f32[512]{0:T(512)S(1)}, f32[512]{0:T(512)}, u32[]{:S(2)}) copy-start(f32[512]{0:T(512)} %copy-done.42) | copy-start | bytes 6148
  377.0 68.8 %copy-start.52 = (f32[768]{0:T(1024)S(1)}, f32[768]{0:T(1024)}, u32[]{:S(2)}) copy-start(f32[768]{0:T(1024)} %get-tuple-element.19) | copy-start | bytes 9220
  377.0 68.8 %copy-start.53 = (f32[768]{0:T(1024)S(1)}, f32[768]{0:T(1024)}, u32[]{:S(2)}) copy-start(f32[768]{0:T(1024)} %get-tuple-element.15) | copy-start | bytes 9220
  377.1 68.8 %copy-start.54 = (f32[768]{0:T(1024)S(1)}, f32[768]{0:T(1024)}, u32[]{:S(2)}) copy-start(f32[768]{0:T(1024)} %get-tuple-element.39) | copy-start | bytes 9220
  377.1 68.8 %copy-start.55 = (f32[768]{0:T(1024)S(1)}, f32[768]{0:T(1024)}, u32[]{:S(2)}) copy-start(f32[768]{0:T(1024)} %get-tuple-element.44) | copy-start | bytes 9220
  441.9 43.0 %copy-start.13 = (bf16[512,768]{1,0:T(8,128)(2,1)S(1)}, bf16[512,768]{1,0:T(8,128)(2,1)}, u32[]{:S(2)}) copy-start(bf16[512,768]{1,0:T(8,128)(2,1)} %reduce-scatter.11.cloned.1.call-done) | copy-start | bytes 2359300
  (61 other events, 368.2 us)
Sparse Core Ops, SparseCore 0:
  12.8 29.8 all-gather.4
  72.1 26.1 reduce-scatter.4
  104.1 27.1 all-gather.6
  132.8 27.1 all-gather.8
  185.5 26.1 reduce-scatter.8
  213.8 26.1 reduce-scatter.6
  245.2 27.1 all-gather.10
  353.5 26.1 reduce-scatter.10
  385.4 257.7 all-reduce.4
where the time goes:
time: 671 us; the launch traced here: 661 us
  waiting for transfers between devices  308 us (46%)
  matrix products  120 us (18%)
  blocking collectives  103 us (15%)
  other arithmetic  65.4 us (10%)
  local copies, waits for them, and re-layouts  39 us (6%)
  between operations  15 us (2%)
  starting transfers between devices  10 us (1%)
    psum x1, waiting for transfers between devices, on_device(): lax.psum((qkv_grad, query_bias_grad, value_bias_grad, out_grad, up_grad,...  157 us
    psum x1, blocking collectives, on_device(): lax.psum((qkv_grad, query_bias_grad, value_bias_grad, out_grad, up_grad,...  64.1 us
    psum x1, blocking collectives, on_device(): lax.psum((first_gain_part, first_shift_part, out_bias_part, second_gain_p...  39 us
    all_gather x1, waiting for transfers between devices, on_device(): lax.all_gather(second_normed.astype(bf16), 'tp', axis=0, tiled=True)  26.7 us
    unnamed x157, local copies, waits for them, and re-layouts  26.6 us
    reduce_scatter x1, waiting for transfers between devices, on_device(): lax.psum_scatter(jnp.dot(attended, out_weight, preferred_element_type=f32...  26 us
    all_gather x1, waiting for transfers between devices, on_device(): grad_attn_rows = lax.all_gather(middle_low, 'tp', axis=0, tiled=True)  25.2 us
    all_gather x1, waiting for transfers between devices, on_device(): lax.all_gather(first_normed.astype(bf16), 'tp', axis=0, tiled=True)  24.4 us
  transfers between devices with their start and end apart: 9, of which 8 were waited for; matrix products, arithmetic and copies ran while one was open for 9% of the time, Pallas kernels for 0%

commit v1 on v0

v1 whole, which is shorter than its diff:
```python
import jax
import jax.numpy as jnp
from jax import lax
from jax.experimental import pallas as pl
from jax.experimental.pallas import tpu as pltpu
from jax.sharding import PartitionSpec as P

HEAD = 64
EPS = 1e-06
MASKED = -1e30
BLK = 256
PAIR = 2 * HEAD
f32 = jnp.float32
bf16 = jnp.bfloat16


def stats(values):
    center = values - jnp.mean(values, axis=-1, keepdims=True)
    spread = jnp.mean(center * center, axis=-1, keepdims=True)
    scale = lax.rsqrt(spread + EPS)
    return center * scale, scale


def dot_nt(left, right):
    return lax.dot_general(left, right, (((1,), (1,)), ((), ())), preferred_element_type=f32)


def dot_nn(left, right):
    return lax.dot_general(left, right, (((1,), (0,)), ((), ())), preferred_element_type=f32)


def dot_tn(left, right):
    return lax.dot_general(left, right, (((0,), (0,)), ((), ())), preferred_element_type=f32)


def meets(lo_ref, hi_ref, i, j):
    return (lo_ref[j] <= hi_ref[i]) & (hi_ref[j] >= lo_ref[i])


def by_head(block):
    lane = lax.broadcasted_iota(jnp.int32, block.shape, 1)
    zero = jnp.zeros_like(block)
    return jnp.where(lane < HEAD, block, zero), jnp.where(lane < HEAD, zero, block)


def attend_kernel(lo_ref, hi_ref, q_ref, k_ref, v_ref, row_ref, col_ref, out_ref, lse_ref, vt_ref, acc_ref, m_ref, l_ref):
    i = pl.program_id(1)
    blocks = k_ref.shape[0] // BLK

    @pl.when(i == 0)
    def _():
        vt_ref[...] = v_ref[...].T

    acc_ref[...] = jnp.zeros_like(acc_ref)
    m_ref[...] = jnp.full_like(m_ref, MASKED)
    l_ref[...] = jnp.zeros_like(l_ref)
    queries = by_head(q_ref[...])
    row_seg = row_ref[0:1, :]

    def step(j, carry):
        @pl.when(meets(lo_ref, hi_ref, i, j))
        def _():
            at = pl.multiple_of(j * BLK, BLK)
            keys = k_ref[pl.ds(at, BLK), :]
            col = col_ref[pl.ds(at, BLK), :]
            same = jnp.concatenate([col] * (BLK // 128), axis=1) == row_seg
            for h in range(2):
                scores = jnp.where(same, dot_nt(keys, queries[h]), MASKED)
                old = m_ref[h : h + 1, :]
                new = jnp.maximum(old, jnp.max(scores, axis=0, keepdims=True))
                fade = jnp.exp(old - new)
                expon = jnp.where(same, jnp.exp(scores - new), 0.0)
                m_ref[h : h + 1, :] = new
                l_ref[h : h + 1, :] = fade * l_ref[h : h + 1, :] + jnp.sum(expon, axis=0, keepdims=True)
                span = slice(h * HEAD, (h + 1) * HEAD)
                acc_ref[span, :] = fade * acc_ref[span, :] + dot_nn(
                    vt_ref[span, pl.ds(at, BLK)], expon.astype(bf16)
                )

        return carry

    lax.fori_loop(0, blocks, step, 0)
    halves = [acc_ref[h * HEAD : (h + 1) * HEAD, :] / l_ref[h : h + 1, :] for h in range(2)]
    out_ref[...] = jnp.concatenate(halves, axis=0).T.astype(bf16)
    lse_ref[...] = jnp.concatenate(
        [m_ref[0:2, :] + jnp.log(l_ref[0:2, :]), jnp.zeros((6, BLK), f32)], axis=0
    )


def attend(qkv, lo, hi, seg_row, seg_col, pairs):
    rows = qkv.shape[0]
    return pl.pallas_call(
        attend_kernel,
        grid_spec=pltpu.PrefetchScalarGridSpec(
            num_scalar_prefetch=2,
            grid=(pairs, rows // BLK),
            in_specs=[
                pl.BlockSpec((BLK, PAIR), lambda p, i, *_: (i, p)),
                pl.BlockSpec((rows, PAIR), lambda p, i, *_: (0, pairs + p)),
                pl.BlockSpec((rows, PAIR), lambda p, i, *_: (0, 2 * pairs + p)),
                pl.BlockSpec((8, BLK), lambda p, i, *_: (0, i)),
                pl.BlockSpec((rows, 128), lambda p, i, *_: (0, 0)),
            ],
            out_specs=[
                pl.BlockSpec((BLK, PAIR), lambda p, i, *_: (i, p)),
                pl.BlockSpec((8, BLK), lambda p, i, *_: (p, i)),
            ],
            scratch_shapes=[
                pltpu.VMEM((PAIR, rows), bf16),
                pltpu.VMEM((PAIR, BLK), f32),
                pltpu.VMEM((8, BLK), f32),
                pltpu.VMEM((8, BLK), f32),
            ],
        ),
        out_shape=[
            jax.ShapeDtypeStruct((rows, pairs * PAIR), bf16),
            jax.ShapeDtypeStruct((8 * pairs, rows), f32),
        ],
        name="attend",
    )(lo, hi, qkv, qkv, qkv, seg_row, seg_col)


def attend_back_kernel(
    lo_ref, hi_ref, q_ref, k_ref, v_ref, g_ref, o_ref, lse_ref, row_ref, col_ref,
    dq_ref, dk_ref, dv_ref, qb_ref, vb_ref, kt_ref, dk_acc, dv_acc, dq_acc,
):
    i = pl.program_id(1)
    blocks = k_ref.shape[0] // BLK

    @pl.when(i == 0)
    def _():
        kt_ref[...] = k_ref[...].T
        dk_acc[...] = jnp.zeros_like(dk_acc)
        dv_acc[...] = jnp.zeros_like(dv_acc)
        qb_ref[...] = jnp.zeros_like(qb_ref)

    dq_acc[...] = jnp.zeros_like(dq_acc)
    queries = by_head(q_ref[...])
    grads = by_head(g_ref[...])
    prod = (g_ref[...].astype(f32) * o_ref[...].astype(f32)).T
    inner = [jnp.sum(prod[h * HEAD : (h + 1) * HEAD], axis=0, keepdims=True) for h in range(2)]
    row_seg = row_ref[0:1, :]

    def step(j, carry):
        @pl.when(meets(lo_ref, hi_ref, i, j))
        def _():
            at = pl.multiple_of(j * BLK, BLK)
            keys = k_ref[pl.ds(at, BLK), :]
            vals = v_ref[pl.ds(at, BLK), :]
            col = col_ref[pl.ds(at, BLK), :]
            same = jnp.concatenate([col] * (BLK // 128), axis=1) == row_seg
            dv_new = dv_acc[pl.ds(at, BLK), :]
            dk_new = dk_acc[pl.ds(at, BLK), :]
            for h in range(2):
                scores = jnp.where(same, dot_nt(keys, queries[h]), MASKED)
                probs = jnp.exp(scores - lse_ref[h : h + 1, :])
                dv_new = dv_new + dot_nn(probs.astype(bf16), grads[h])
                back = (probs * (dot_nt(vals, grads[h]) - inner[h])).astype(bf16)
                dk_new = dk_new + dot_nn(back, queries[h])
                span = slice(h * HEAD, (h + 1) * HEAD)
                dq_acc[span, :] += dot_nn(kt_ref[span, pl.ds(at, BLK)], back)
            dv_acc[pl.ds(at, BLK), :] = dv_new
            dk_acc[pl.ds(at, BLK), :] = dk_new

        return carry

    lax.fori_loop(0, blocks, step, 0)
    dq = dq_acc[...].T * HEAD ** (-0.5)
    dq_ref[...] = dq.astype(bf16)
    qb_ref[0:1, :] += jnp.sum(dq, axis=0, keepdims=True)

    @pl.when(i == pl.num_programs(1) - 1)
    def _():
        dk_ref[...] = dk_acc[...].astype(bf16)
        dv = dv_acc[...]
        dv_ref[...] = dv.astype(bf16)
        vb_ref[...] = jnp.broadcast_to(jnp.sum(dv, axis=0, keepdims=True), vb_ref.shape)


def attend_back(qkv, grads, attended, lse, lo, hi, seg_row, seg_col, pairs):
    rows = qkv.shape[0]
    wide = pairs * PAIR
    return pl.pallas_call(
        attend_back_kernel,
        grid_spec=pltpu.PrefetchScalarGridSpec(
            num_scalar_prefetch=2,
            grid=(pairs, rows // BLK),
            in_specs=[
                pl.BlockSpec((BLK, PAIR), lambda p, i, *_: (i, p)),
                pl.BlockSpec((rows, PAIR), lambda p, i, *_: (0, pairs + p)),
                pl.BlockSpec((rows, PAIR), lambda p, i, *_: (0, 2 * pairs + p)),
                pl.BlockSpec((BLK, PAIR), lambda p, i, *_: (i, p)),
                pl.BlockSpec((BLK, PAIR), lambda p, i, *_: (i, p)),
                pl.BlockSpec((8, BLK), lambda p, i, *_: (p, i)),
                pl.BlockSpec((8, BLK), lambda p, i, *_: (0, i)),
                pl.BlockSpec((rows, 128), lambda p, i, *_: (0, 0)),
            ],
            out_specs=[
                pl.BlockSpec((BLK, PAIR), lambda p, i, *_: (i, p)),
                pl.BlockSpec((rows, PAIR), lambda p, i, *_: (0, p)),
                pl.BlockSpec((rows, PAIR), lambda p, i, *_: (0, p)),
                pl.BlockSpec((8, PAIR), lambda p, i, *_: (0, p)),
                pl.BlockSpec((8, PAIR), lambda p, i, *_: (0, p)),
            ],
            scratch_shapes=[
                pltpu.VMEM((PAIR, rows), bf16),
                pltpu.VMEM((rows, PAIR), f32),
                pltpu.VMEM((rows, PAIR), f32),
                pltpu.VMEM((PAIR, BLK), f32),
            ],
        ),
        out_shape=[
            jax.ShapeDtypeStruct((rows, wide), bf16),
            jax.ShapeDtypeStruct((rows, wide), bf16),
            jax.ShapeDtypeStruct((rows, wide), bf16),
            jax.ShapeDtypeStruct((8, wide), f32),
            jax.ShapeDtypeStruct((8, wide), f32),
        ],
        name="attend_back",
    )(lo, hi, qkv, qkv, qkv, grads, attended, lse, seg_row, seg_col)


def make(n_dp):
    bits = n_dp.bit_length() - 1

    def swap_tp(value):
        return lax.ppermute(value, "tp", [(0, 1), (1, 0)])

    def swap_dp(value, bit):
        return lax.ppermute(value, "dp", [(d, d ^ (1 << bit)) for d in range(n_dp)])

    def reduce_dp(value, order):
        spot = lax.axis_index("dp")
        for bit in order:
            half = value.shape[0] // 2
            mine = (spot >> bit) & 1
            sent = lax.dynamic_slice_in_dim(value, (1 - mine) * half, half, 0)
            kept = lax.dynamic_slice_in_dim(value, mine * half, half, 0)
            value = (kept.astype(f32) + swap_dp(sent, bit).astype(f32)).astype(bf16)
        for bit in reversed(order):
            mine = ((spot >> bit) & 1) == 0
            came = swap_dp(value, bit)
            value = jnp.concatenate(
                [jnp.where(mine, value, came), jnp.where(mine, came, value)], axis=0
            )
        return value

    def small_sum(value, with_tp):
        if with_tp:
            value = value + swap_tp(value)
        for bit in range(bits):
            value = value + swap_dp(value, bit)
        return value

    order = list(range(bits))

    def on_device(
        tokens, segment_ids, first_gain, first_shift, qkv_weight, query_bias, value_bias, out_weight,
        out_bias, second_gain, second_shift, up_weight, up_bias, down_weight, down_bias, grad_out,
    ):
        width = tokens.shape[1]
        local = qkv_weight.shape[2]
        rows = segment_ids.shape[0]
        own = rows // 2
        pairs = local // PAIR
        qkv_flat = qkv_weight.reshape(width, 3 * local)

        def other(value):
            return swap_tp(value)

        tokens_all = jnp.concatenate([tokens, other(tokens)], axis=0)
        grad_all = jnp.concatenate([grad_out, other(grad_out)], axis=0)
        here = lax.axis_index("tp")
        segs = jnp.where(here == 0, segment_ids, jnp.roll(segment_ids, own))
        seg_row = jnp.broadcast_to(segs[None, :], (8, rows))
        seg_col = jnp.broadcast_to(segs[:, None], (rows, 128))
        blocked = segs.reshape(rows // BLK, BLK)
        lo, hi = blocked[:, 0], blocked[:, BLK - 1]

        first_z, first_scale = stats(tokens_all.astype(f32))
        first_low = (first_z * first_gain + first_shift).astype(bf16)
        bias = jnp.concatenate([query_bias, jnp.zeros_like(query_bias), value_bias])
        size = jnp.concatenate([jnp.full((local,), HEAD ** (-0.5), f32), jnp.ones((2 * local,), f32)])
        qkv = ((dot_nn(first_low, qkv_flat) + bias) * size).astype(bf16)
        attended, lse = attend(qkv, lo, hi, seg_row, seg_col, pairs)
        out_there = dot_nn(attended[own:], out_weight).astype(bf16)
        out_here = dot_nn(attended[:own], out_weight)
        middle = tokens.astype(f32) + (out_here + other(out_there).astype(f32)) + out_bias
        second_z, second_scale = stats(middle)
        second_own = (second_z * second_gain + second_shift).astype(bf16)
        second_low = jnp.concatenate([second_own, other(second_own)], axis=0)
        pre_act = dot_nn(second_low, up_weight) + up_bias
        below = 0.5 * (1.0 + lax.erf(pre_act * 0.5**0.5))
        slope = (below + pre_act * (jnp.exp(-0.5 * pre_act * pre_act) * (0.5 / jnp.pi) ** 0.5)).astype(bf16)
        hidden = (pre_act * below).astype(bf16)
        pre_grad = dot_nt(grad_all, down_weight) * slope.astype(f32)
        up_bias_part = jnp.sum(pre_grad, axis=0)
        pre_low = pre_grad.astype(bf16)
        back_there = dot_nt(pre_low[own:], up_weight).astype(bf16)
        back_here = dot_nt(pre_low[:own], up_weight)
        second_back = back_here + other(back_there).astype(f32)

        down_there = dot_nn(hidden[own:], down_weight).astype(bf16)
        down_here = dot_nn(hidden[:own], down_weight)
        layer_out = (middle + (down_here + other(down_there).astype(f32)) + down_bias).astype(bf16)
        down_grad = reduce_dp(dot_tn(hidden, grad_all).astype(bf16), order)
        up_grad = reduce_dp(dot_tn(second_low, pre_low).astype(bf16), order)

        def norm_back(back, gain, z, scale):
            scaled = back * gain
            return scale * (
                scaled
                - jnp.mean(scaled, axis=-1, keepdims=True)
                - z * jnp.mean(scaled * z, axis=-1, keepdims=True)
            )

        grad_f = grad_out.astype(f32)
        middle_grad = grad_f + norm_back(second_back, second_gain, second_z, second_scale)
        second_gain_part = jnp.sum(second_back * second_z, axis=0)
        second_shift_part = jnp.sum(second_back, axis=0)
        out_bias_part = jnp.sum(middle_grad, axis=0)
        down_bias_part = jnp.sum(grad_f, axis=0)
        middle_own = middle_grad.astype(bf16)
        middle_all = jnp.concatenate([middle_own, other(middle_own)], axis=0)
        out_grad = reduce_dp(dot_tn(attended, middle_all).astype(bf16), order)
        attended_grad = dot_nt(middle_all, out_weight).astype(bf16)
        dq, dk, dv, query_bias_part, value_bias_part = attend_back(
            qkv, attended_grad, attended, lse, lo, hi, seg_row, seg_col, pairs
        )
        proj_grad = jnp.concatenate([dq, dk, dv], axis=1)
        first_back_part = dot_nt(proj_grad, qkv_flat)
        first_there = first_back_part[own:].astype(bf16)
        first_back = first_back_part[:own] + other(first_there).astype(f32)
        qkv_grad = reduce_dp(dot_tn(first_low, proj_grad).astype(bf16), order)
        first_gain_part = jnp.sum(first_back_part * first_z, axis=0)
        first_shift_part = jnp.sum(first_back_part, axis=0)
        tokens_grad = (
            middle_grad + norm_back(first_back, first_gain, first_z[:own], first_scale[:own])
        ).astype(bf16)
        both = small_sum(
            jnp.stack(
                [
                    first_gain_part, first_shift_part, out_bias_part,
                    second_gain_part, second_shift_part, down_bias_part,
                ]
            ),
            True,
        )
        split = small_sum(
            jnp.concatenate([query_bias_part[0], value_bias_part[0], up_bias_part]).reshape(-1, width),
            False,
        ).reshape(-1)
        return (
            layer_out,
            tokens_grad,
            both[0],
            both[1],
            qkv_grad.astype(f32).reshape(width, 3, local),
            split[:local],
            split[local : 2 * local],
            out_grad.astype(f32),
            both[2],
            both[3],
            both[4],
            up_grad.astype(f32),
            split[2 * local :],
            down_grad.astype(f32),
            both[5],
        )

    return on_device


def solution(mesh):
    rows, whole, tp = P(("dp", "tp"), None), P(), P("tp")
    in_specs = (
        rows, P("dp"), whole, whole, P(None, None, "tp"), tp, tp, P("tp", None),
        whole, whole, whole, P(None, "tp"), tp, P("tp", None), whole, rows,
    )
    out_specs = (
        rows, rows, whole, whole, P(None, None, "tp"), tp, tp, P("tp", None),
        whole, whole, whole, P(None, "tp"), tp, P("tp", None), whole,
    )
    return jax.shard_map(
        make(mesh.shape["dp"]), mesh=mesh, in_specs=in_specs, out_specs=out_specs, check_vma=False
    )
```

time: 671 us -> 384 us (0.57); the launches traced: 661 us -> 382 us
  waiting for transfers between devices: 308 us -> 163 us
  blocking collectives: 103 us -> 0 us
  matrix products: 120 us -> 45.5 us
  starting transfers between devices: 10 us -> 65.7 us
  Pallas kernels: 0 us -> 51.2 us
  other arithmetic: 65.4 us -> 25.6 us
  between operations: 15 us -> 1.82 us
  local copies, waits for them, and re-layouts: 39 us -> 29.4 us
    ppermute x0 -> x49, waiting for transfers between devices: none -> 163 us  [the longest x9 92.2 us: swap_tp(): return lax.ppermute(value, 'tp', [(0, 1), (1, 0)])]
    psum x1 -> x0, waiting for transfers between devices: 157 us -> none  [on_device(): lax.psum((qkv_grad, query_bias_grad, value_bias_grad, out_grad, up_grad,...]
    psum x2 -> x0, blocking collectives: 103 us -> none  [the longest x1 64.1 us: on_device(): lax.psum((qkv_grad, query_bias_grad, value_bias_grad, out_grad, up_grad,...]
    all_gather x4 -> x0, waiting for transfers between devices: 97.4 us -> none  [the longest x1 26.7 us: on_device(): lax.all_gather(second_normed.astype(bf16), 'tp', axis=0, tiled=True)]
    dot_general x24 -> x15, matrix products: 120 us -> 45.5 us  [the longest x6 16.5 us: dot_nn(): lax.dot_general(left, right, (((1,), (0,)), ((), ())), preferred_element_...]
    ppermute x0 -> x49, starting transfers between devices: none -> 65.7 us  [the longest x40 51.5 us: swap_dp(): return lax.ppermute(value, 'dp', [(d, d ^ 1 << bit) for d in range(n_dp)])]
    reduce_scatter x4 -> x0, waiting for transfers between devices: 53.4 us -> none  [the longest x1 26 us: on_device(): lax.psum_scatter(jnp.dot(attended, out_weight, preferred_element_type=f32...]
    pallas_call x0 -> x2, Pallas kernels: none -> 51.2 us  [the longest x1 27.8 us: attend_back(): pl.pallas_call(attend_back_kernel, grid_spec=pltpu.PrefetchScalarGridSpec...]
  transfers between devices with their start and end apart: 9 -> 49, of which waited for: 8 -> 24; matrix products, arithmetic and copies ran while one was open for 9% -> 17% of each run, Pallas kernels for 0% -> 7%
where the time goes in v1:
time: 384 us; the launch traced here: 382 us
  waiting for transfers between devices  163 us (42%)
  starting transfers between devices  65.7 us (17%)
  Pallas kernels  51.2 us (13%)
  matrix products  45.5 us (12%)
  local copies, waits for them, and re-layouts  29.4 us (8%)
  other arithmetic  25.6 us (7%)
    ppermute x9, waiting for transfers between devices, swap_tp(): return lax.ppermute(value, 'tp', [(0, 1), (1, 0)])  92.2 us
    ppermute x40, waiting for transfers between devices, swap_dp(): return lax.ppermute(value, 'dp', [(d, d ^ 1 << bit) for d in range(n_dp)])  71 us
    ppermute x40, starting transfers between devices, swap_dp(): return lax.ppermute(value, 'dp', [(d, d ^ 1 << bit) for d in range(n_dp)])  51.5 us
    pallas_call x1, Pallas kernels, attend_back(): pl.pallas_call(attend_back_kernel, grid_spec=pltpu.PrefetchScalarGridSpec...  27.8 us
    pallas_call x1, Pallas kernels, attend(): pl.pallas_call(attend_kernel, grid_spec=pltpu.PrefetchScalarGridSpec(num_...  23.4 us
    dot_general x6, matrix products, dot_nn(): lax.dot_general(left, right, (((1,), (0,)), ((), ())), preferred_element_...  16.5 us
    dot_general x5, matrix products, dot_nt(): lax.dot_general(left, right, (((1,), (1,)), ((), ())), preferred_element_...  15.9 us
    ppermute x9, starting transfers between devices, swap_tp(): return lax.ppermute(value, 'tp', [(0, 1), (1, 0)])  14.2 us
  transfers between devices with their start and end apart: 49, of which 24 were waited for; matrix products, arithmetic and copies ran while one was open for 17% of the time, Pallas kernels for 7%

profile of v1, /device:TPU:0, one launch (start us, length us, event | category | flops | bytes accessed | tf_op | source)
XLA Modules:
  0.0 382.3 jit_solution(6540356839653016210)
XLA Ops:
  5.2 3.9 %copy.37 = bf16[768,3,384]{0,2,1:T(8,128)(2,1)} copy(bf16[768,3,384]{2,0,1:T(8,128)(2,1)} %param.20) | data formatting | bytes 3538944 | tf_op args[4]
  9.8 11.7 %collective-permute-done = bf16[512,768]{1,0:T(8,128)(2,1)} collective-permute-done((bf16[512,768]{1,0:T(8,128)(2,1)}, bf16[512,768]{1,0:T(8,128)(2,1)}, u32[]{:S(2)}, u32[]{:S(2)}) %collective-permute-start) | collective-permute-done | bytes 786464 | tf_op jit(solution)/shard_map/ppermute | solution.py:227
  24.8 5.1 %multiply_convert_fusion.1.q_ref.k_ref.v_ref = bf16[1024,1152]{1,0:T(8,128)(2,1)} fusion(bf16[768,1152]{0,1:T(8,128)(2,1)S(1)} %bitcast.23, f32[1152]{0:T(1024)S(1)} %copy-done.39, f32[1152]{0:T(1024)S(1)} %pad_maximum_fusion.20, f32[768]{0:T(1024)S(1)} %copy-done.38, f32[768]{0:T(1024)S(1)} %copy-done.27, f32[1024]{0:T(1024)S(1)} %add_rsqrt_fusion, ...), kind=kOutput, calls=%fused_computation.9 | convolution fusion | flops 1822556160 | bytes 5725184 | tf_op jit(solution)/shard_map/dot_general | solution.py:29
  31.5 23.4 %attend.1 = (bf16[1024,384]{1,0:T(8,128)(2,1)}, f32[24,1024]{1,0:T(8,128)}) custom-call(s32[4]{0:T(128)} %get-tuple-element.74.lo_ref, s32[4]{0:T(128)} %get-tuple-element.73.hi_ref, bf16[1024,1152]{1,0:T(8,128)(2,1)} %multiply_convert_fusion.1.q_ref.k_ref.v_ref, bf16[1024,1152]{1,0:T(8,128)(2,1)} %multiply_convert_fusion.1.q_ref.k_ref.v_ref, ...), custom_call_target="tpu_custom_call" | custom-call | tf_op jit(solution)/shard_map/attend/pallas_call | solution.py:92
  58.9 15.8 %collective-permute-done.1 = bf16[512,768]{1,0:T(8,128)(2,1)S(1)} collective-permute-done((bf16[512,768]{1,0:T(8,128)(2,1)S(1)}, bf16[512,768]{1,0:T(8,128)(2,1)S(1)}, u32[]{:S(2)}, u32[]{:S(2)}) %collective-permute-start.1) | collective-permute-done | bytes 786464 | tf_op jit(solution)/shard_map/ppermute | solution.py:227
  80.1 11.5 %collective-permute-done.4 = bf16[512,768]{1,0:T(8,128)(2,1)} collective-permute-done((bf16[512,768]{1,0:T(8,128)(2,1)}, bf16[512,768]{1,0:T(8,128)(2,1)}, u32[]{:S(2)}, u32[]{:S(2)}) %collective-permute-start.4) | collective-permute-done | bytes 786464 | tf_op jit(solution)/shard_map/ppermute | solution.py:227
  92.8 15.7 %collective-permute-done.2 = bf16[512,768]{1,0:T(8,128)(2,1)} collective-permute-done((bf16[512,768]{1,0:T(8,128)(2,1)}, bf16[512,768]{1,0:T(8,128)(2,1)}, u32[]{:S(2)}, u32[]{:S(2)}) %collective-permute-start.2) | collective-permute-done | bytes 786464 | tf_op jit(solution)/shard_map/ppermute | solution.py:227
  108.5 4.7 %multiply_convert_fusion = (bf16[1024,1536]{1,0:T(8,128)(2,1)S(1)}, f32[1024,1536]{1,0:T(8,128)S(1)}) fusion(f32[1536]{0:T(1024)S(1)} %copy-done.36, bf16[768,1536]{1,0:T(8,128)(2,1)S(1)} %copy-done, bf16[512,768]{1,0:T(8,128)(2,1)} %collective-permute-done.2, bf16[512,768]{1,0:T(8,128)(2,1)} %add_convert_fusion.6), kind=kOutput, calls=%fused_computation.7 | convolution fusion | flops 2428502016 | bytes 13375488 | tf_op jit(solution)/shard_map/dot_general | solution.py:29
  113.2 5.6 %fusion.39 = (f32[1536]{0:T(1024)S(1)}, bf16[1024,1536]{1,0:T(8,128)(2,1)S(1)}) fusion(f32[1024,1536]{1,0:T(8,128)S(1)} %get-tuple-element.123, f32[1536]{0:T(1024)S(1)} %copy-done.36, bf16[1024,768]{1,0:T(8,128)(2,1)S(1)} %constant_dynamic-update-slice_fusion, bf16[1536,768]{1,0:T(8,128)(2,1)S(1)} %copy-done.34), kind=kOutput, calls=%fused_computation.170 | convolution fusion | flops 2437937664 | bytes 13381632 | tf_op jit(solution)/shard_map/dot_general | solution.py:25
  123.8 4.3 %convolution_convert_fusion.1 = bf16[768,1536]{1,0:T(8,128)(2,1)S(1)} fusion(bf16[1024,1536]{1,0:T(8,128)(2,1)S(1)} %get-tuple-element.78, bf16[512,768]{1,0:T(8,128)(2,1)} %collective-permute-done.2, bf16[512,768]{1,0:T(8,128)(2,1)} %add_convert_fusion.6), kind=kOutput, calls=%fused_computation.15 | convolution fusion | flops 2420244480 | bytes 7077888 | tf_op jit(solution)/shard_map/dot_general | solution.py:33
  133.5 24.1 %collective-permute-done.5 = bf16[512,768]{1,0:T(8,128)(2,1)S(1)} collective-permute-done((bf16[512,768]{1,0:T(8,128)(2,1)S(1)}, bf16[512,768]{1,0:T(8,128)(2,1)S(1)}, u32[]{:S(2)}, u32[]{:S(2)}) %collective-permute-start.5) | collective-permute-done | bytes 786464 | tf_op jit(solution)/shard_map/ppermute | solution.py:227
  169.2 13.5 %collective-permute-done.6 = bf16[512,768]{1,0:T(8,128)(2,1)S(1)} collective-permute-done((bf16[512,768]{1,0:T(8,128)(2,1)S(1)}, bf16[512,768]{1,0:T(8,128)(2,1)S(1)}, u32[]{:S(2)}, u32[]{:S(2)}) %collective-permute-start.6) | collective-permute-done | bytes 786464 | tf_op jit(solution)/shard_map/ppermute | solution.py:227
  184.6 27.8 %attend_back.1 = (bf16[1024,384]{1,0:T(8,128)(2,1)}, bf16[1024,384]{1,0:T(8,128)(2,1)}, bf16[1024,384]{1,0:T(8,128)(2,1)}, f32[8,384]{1,0:T(8,128)}, f32[8,384]{1,0:T(8,128)}) custom-call(s32[4]{0:T(128)} %get-tuple-element.74.lo_ref, s32[4]{0:T(128)} %get-tuple-element.73.hi_ref, bf16[1024,1152]{1,0:T(8,128)(2,1)} %multiply_convert_fusion.1.q_ref.k_ref.v_ref, ...), custom_call_target="tpu_custom_call" | custom-call | tf_op jit(solution)/shard_map/attend_back/pallas_call | solution.py:183
  214.0 5.4 %collective-permute-start.21 = (f32[3,768]{1,0:T(4,128)S(1)}, f32[3,768]{1,0:T(4,128)S(1)}, u32[]{:S(2)}, u32[]{:S(2)}) collective-permute-start(f32[3,768]{1,0:T(4,128)S(1)} %reshape.113), channel_id=1, source_target_pairs={{0,2},{2,0},{4,6},{6,4},{8,10},{10,8},{12,14},{14,12},{16,18},{18,... | collective-permute-start | bytes 27656 | tf_op jit(solution)/shard_map/ppermute | solution.py:230
  222.1 5.1 %fusion.37 = (f32[768]{0:T(1024)S(1)}, f32[768]{0:T(1024)S(1)}, f32[1024,768]{1,0:T(8,128)}, f32[1024,768]{1,0:T(8,128)}) fusion(f32[1024]{0:T(1024)S(1)} %add_rsqrt_fusion, f32[1024]{0:T(1024)S(1)} %broadcast_multiply_fusion, bf16[512,768]{1,0:T(8,128)(2,1)} %collective-permute-done, bf16[512,768]{1,0:T(8,128)(2,1)S(1)} %copy-done.4, ...), kind=kOutput, calls=%fused_computation.168 | convolution fusion | flops 1819015680 | bytes 12007424 | tf_op jit(solution)/shard_map/dot_general | solution.py:25
  235.3 10.0 %collective-permute-start.23 = (f32[3,768]{1,0:T(4,128)S(1)}, f32[3,768]{1,0:T(4,128)S(1)}, u32[]{:S(2)}, u32[]{:S(2)}) collective-permute-start(f32[3,768]{1,0:T(4,128)S(1)} %add.308), channel_id=1, source_target_pairs={{0,8},{2,10},{4,12},{6,14},{8,0},{10,2},{12,4},{14,6},{16,24},{18,... | collective-permute-start | bytes 27656 | tf_op jit(solution)/shard_map/ppermute | solution.py:230
  274.8 9.2 %collective-permute-done.27 = bf16[48,768]{1,0:T(8,128)(2,1)S(1)} collective-permute-done((bf16[48,768]{1,0:T(8,128)(2,1)S(1)}, bf16[48,768]{1,0:T(8,128)(2,1)S(1)}, u32[]{:S(2)}, u32[]{:S(2)}) %collective-permute-start.27) | collective-permute-done | bytes 73760 | tf_op jit(solution)/shard_map/ppermute | solution.py:230
  284.2 4.8 %collective-permute-done.28 = bf16[24,768]{1,0:T(8,128)(2,1)S(1)} collective-permute-done((bf16[24,768]{1,0:T(8,128)(2,1)S(1)}, bf16[24,768]{1,0:T(8,128)(2,1)S(1)}, u32[]{:S(2)}, u32[]{:S(2)}) %collective-permute-start.28) | collective-permute-done | bytes 36896 | tf_op jit(solution)/shard_map/ppermute | solution.py:230
  297.0 6.8 %collective-permute-done.44 = bf16[96,768]{1,0:T(8,128)(2,1)S(1)} collective-permute-done((bf16[96,768]{1,0:T(8,128)(2,1)S(1)}, bf16[96,768]{1,0:T(8,128)(2,1)S(1)}, u32[]{:S(2)}, u32[]{:S(2)}) %collective-permute-start.44) | collective-permute-done | bytes 147488 | tf_op jit(solution)/shard_map/ppermute | solution.py:230
  319.5 8.7 %collective-permute-done.14 = bf16[192,1152]{1,0:T(8,128)(2,1)S(1)} collective-permute-done((bf16[192,1152]{1,0:T(8,128)(2,1)S(1)}, bf16[192,1152]{1,0:T(8,128)(2,1)S(1)}, u32[]{:S(2)}, u32[]{:S(2)}) %collective-permute-start.14) | collective-permute-done | bytes 442400 | tf_op jit(solution)/shard_map/ppermute | solution.py:230
  337.9 4.7 %collective-permute-done.16 = bf16[48,1152]{1,0:T(8,128)(2,1)S(1)} collective-permute-done((bf16[48,1152]{1,0:T(8,128)(2,1)S(1)}, bf16[48,1152]{1,0:T(8,128)(2,1)S(1)}, u32[]{:S(2)}, u32[]{:S(2)}) %collective-permute-start.16) | collective-permute-done | bytes 110624 | tf_op jit(solution)/shard_map/ppermute | solution.py:230
  344.7 4.8 %collective-permute-done.17 = bf16[48,1152]{1,0:T(8,128)(2,1)S(1)} collective-permute-done((bf16[48,1152]{1,0:T(8,128)(2,1)S(1)}, bf16[48,1152]{1,0:T(8,128)(2,1)S(1)}, u32[]{:S(2)}, u32[]{:S(2)}) %collective-permute-start.17) | collective-permute-done | bytes 110624 | tf_op jit(solution)/shard_map/ppermute | solution.py:230
  356.1 10.1 %collective-permute-done.19 = bf16[192,1152]{1,0:T(8,128)(2,1)S(1)} collective-permute-done((bf16[192,1152]{1,0:T(8,128)(2,1)S(1)}, bf16[192,1152]{1,0:T(8,128)(2,1)S(1)}, u32[]{:S(2)}, u32[]{:S(2)}) %collective-permute-start.19) | collective-permute-done | bytes 442400 | tf_op jit(solution)/shard_map/ppermute | solution.py:230
  377.0 5.3 %copy.40 = f32[768,3,384]{2,0,1:T(8,128)} copy(f32[768,3,384]{0,2,1:T(8,128)} %maximum_convert_fusion.2) | data formatting | bytes 7077888
  (294 shorter events, 138.6 us)
Async XLA Ops:
  0.7 20.9 %collective-permute-start = (bf16[512,768]{1,0:T(8,128)(2,1)}, bf16[512,768]{1,0:T(8,128)(2,1)}, u32[]{:S(2)}, u32[]{:S(2)}) collective-permute-start(bf16[512,768]{1,0:T(8,128)(2,1)} %param.16), channel_id=1, source_target_pairs={{0,1},{1,0},{2,3},{3,2},{4,5},{5,4},{6,7},{7,6},{8,9},{9,8},{10,11... | collective-permute-start | bytes 2359304 | tf_op jit(solution)/shard_map/ppermute | solution.py:227
  56.8 17.9 %collective-permute-start.1 = (bf16[512,768]{1,0:T(8,128)(2,1)S(1)}, bf16[512,768]{1,0:T(8,128)(2,1)S(1)}, u32[]{:S(2)}, u32[]{:S(2)}) collective-permute-start(bf16[512,768]{1,0:T(8,128)(2,1)S(1)} %convolution_convert_fusion.4), channel_id=1, source_target_pairs={{0,1},{1,0},{2,3},{3,2},{4,5},{5,4},{6,7},{7,6},{8,9},{9,8},{10,11... | collective-permute-start | bytes 2359304 | tf_op jit(solution)/shard_map/ppermute | solution.py:227
  58.6 33.0 %collective-permute-start.4 = (bf16[512,768]{1,0:T(8,128)(2,1)}, bf16[512,768]{1,0:T(8,128)(2,1)}, u32[]{:S(2)}, u32[]{:S(2)}) collective-permute-start(bf16[512,768]{1,0:T(8,128)(2,1)} %param.31), channel_id=1, source_target_pairs={{0,1},{1,0},{2,3},{3,2},{4,5},{5,4},{6,7},{7,6},{8,9},{9,8},{10,11... | collective-permute-start | bytes 2359304 | tf_op jit(solution)/shard_map/ppermute | solution.py:227
  77.0 31.5 %collective-permute-start.2 = (bf16[512,768]{1,0:T(8,128)(2,1)}, bf16[512,768]{1,0:T(8,128)(2,1)}, u32[]{:S(2)}, u32[]{:S(2)}) collective-permute-start(bf16[512,768]{1,0:T(8,128)(2,1)} %add_convert_fusion.6), channel_id=1, source_target_pairs={{0,1},{1,0},{2,3},{3,2},{4,5},{5,4},{6,7},{7,6},{8,9},{9,8},{10,11... | collective-permute-start | bytes 2359304 | tf_op jit(solution)/shard_map/ppermute | solution.py:227
  121.7 37.8 %collective-permute-start.3 = (bf16[512,768]{1,0:T(8,128)(2,1)S(1)}, bf16[512,768]{1,0:T(8,128)(2,1)S(1)}, u32[]{:S(2)}, u32[]{:S(2)}) collective-permute-start(bf16[512,768]{1,0:T(8,128)(2,1)S(1)} %fusion.17), channel_id=1, source_target_pairs={{0,1},{1,0},{2,3},{3,2},{4,5},{5,4},{6,7},{7,6},{8,9},{9,8},{10,11... | collective-permute-start | bytes 2359304 | tf_op jit(solution)/shard_map/ppermute | solution.py:227
  123.7 33.9 %collective-permute-start.5 = (bf16[512,768]{1,0:T(8,128)(2,1)S(1)}, bf16[512,768]{1,0:T(8,128)(2,1)S(1)}, u32[]{:S(2)}, u32[]{:S(2)}) collective-permute-start(bf16[512,768]{1,0:T(8,128)(2,1)S(1)} %fusion.20), channel_id=1, source_target_pairs={{0,1},{1,0},{2,3},{3,2},{4,5},{5,4},{6,7},{7,6},{8,9},{9,8},{10,11... | collective-permute-start | bytes 2359304 | tf_op jit(solution)/shard_map/ppermute | solution.py:227
  128.2 36.4 %collective-permute-start.33 = (bf16[384,1536]{1,0:T(8,128)(2,1)S(1)}, bf16[384,1536]{1,0:T(8,128)(2,1)S(1)}, u32[]{:S(2)}, u32[]{:S(2)}) collective-permute-start(bf16[384,1536]{1,0:T(8,128)(2,1)S(1)} %constant_dynamic-slice_fusion.7), channel_id=1, source_target_pairs={{0,2},{2,0},{4,6},{6,4},{8,10},{10,8},{12,14},{14,12},{16,18},{18,... | collective-permute-start | bytes 3538952 | tf_op jit(solution)/shard_map/ppermute | solution.py:230
  133.2 33.0 %collective-permute-start.41 = (bf16[768,768]{1,0:T(8,128)(2,1)S(1)}, bf16[768,768]{1,0:T(8,128)(2,1)S(1)}, u32[]{:S(2)}, u32[]{:S(2)}) collective-permute-start(bf16[768,768]{1,0:T(8,128)(2,1)S(1)} %constant_dynamic-slice_fusion.3), channel_id=1, source_target_pairs={{0,2},{2,0},{4,6},{6,4},{8,10},{10,8},{12,14},{14,12},{16,18},{18,... | collective-permute-start | bytes 3538952 | tf_op jit(solution)/shard_map/ppermute | solution.py:230
  162.4 20.3 %collective-permute-start.6 = (bf16[512,768]{1,0:T(8,128)(2,1)S(1)}, bf16[512,768]{1,0:T(8,128)(2,1)S(1)}, u32[]{:S(2)}, u32[]{:S(2)}) collective-permute-start(bf16[512,768]{1,0:T(8,128)(2,1)S(1)} %convert_element_type.250), channel_id=1, source_target_pairs={{0,1},{1,0},{2,3},{3,2},{4,5},{5,4},{6,7},{7,6},{8,9},{9,8},{10,11... | collective-permute-start | bytes 2359304 | tf_op jit(solution)/shard_map/ppermute | solution.py:227
  165.9 97.6 %collective-permute-start.34 = (bf16[192,1536]{1,0:T(8,128)(2,1)}, bf16[192,1536]{1,0:T(8,128)(2,1)}, u32[]{:S(2)}, u32[]{:S(2)}) collective-permute-start(bf16[192,1536]{1,0:T(8,128)(2,1)} %constant_dynamic-slice_fusion.6), channel_id=1, source_target_pairs={{0,4},{2,6},{4,0},{6,2},{8,12},{10,14},{12,8},{14,10},{16,20},{18,... | collective-permute-start | bytes 1769480 | tf_op jit(solution)/shard_map/ppermute | solution.py:230
  167.5 102.3 %collective-permute-start.42 = (bf16[384,768]{1,0:T(8,128)(2,1)}, bf16[384,768]{1,0:T(8,128)(2,1)}, u32[]{:S(2)}, u32[]{:S(2)}) collective-permute-start(bf16[384,768]{1,0:T(8,128)(2,1)} %constant_dynamic-slice_fusion.2), channel_id=1, source_target_pairs={{0,4},{2,6},{4,0},{6,2},{8,12},{10,14},{12,8},{14,10},{16,20},{18,... | collective-permute-start | bytes 1769480 | tf_op jit(solution)/shard_map/ppermute | solution.py:230
  214.0 17.6 %collective-permute-start.21 = (f32[3,768]{1,0:T(4,128)S(1)}, f32[3,768]{1,0:T(4,128)S(1)}, u32[]{:S(2)}, u32[]{:S(2)}) collective-permute-start(f32[3,768]{1,0:T(4,128)S(1)} %reshape.113), channel_id=1, source_target_pairs={{0,2},{2,0},{4,6},{6,4},{8,10},{10,8},{12,14},{14,12},{16,18},{18,... | collective-permute-start | bytes 27656 | tf_op jit(solution)/shard_map/ppermute | solution.py:230
  231.7 13.6 %collective-permute-start.9 = (f32[6,768]{1,0:T(8,128)S(1)}, f32[6,768]{1,0:T(8,128)S(1)}, u32[]{:S(2)}, u32[]{:S(2)}) collective-permute-start(f32[6,768]{1,0:T(8,128)S(1)} %add.290), channel_id=1, source_target_pairs={{0,2},{2,0},{4,6},{6,4},{8,10},{10,8},{12,14},{14,12},{16,18},{18,... | collective-permute-start | bytes 55304 | tf_op jit(solution)/shard_map/ppermute | solution.py:230
  232.5 34.0 %collective-permute-start.25 = (bf16[192,768]{1,0:T(8,128)(2,1)}, bf16[192,768]{1,0:T(8,128)(2,1)}, u32[]{:S(2)}, u32[]{:S(2)}) collective-permute-start(bf16[192,768]{1,0:T(8,128)(2,1)} %constant_dynamic-slice_fusion.11), channel_id=1, source_target_pairs={{0,2},{2,0},{4,6},{6,4},{8,10},{10,8},{12,14},{14,12},{16,18},{18,... | collective-permute-start | bytes 884744 | tf_op jit(solution)/shard_map/ppermute | solution.py:230
  235.3 13.8 %collective-permute-start.23 = (f32[3,768]{1,0:T(4,128)S(1)}, f32[3,768]{1,0:T(4,128)S(1)}, u32[]{:S(2)}, u32[]{:S(2)}) collective-permute-start(f32[3,768]{1,0:T(4,128)S(1)} %add.308), channel_id=1, source_target_pairs={{0,8},{2,10},{4,12},{6,14},{8,0},{10,2},{12,4},{14,6},{16,24},{18,... | collective-permute-start | bytes 27656 | tf_op jit(solution)/shard_map/ppermute | solution.py:230
  256.5 57.1 %collective-permute-start.13 = (bf16[384,1152]{1,0:T(8,128)(2,1)}, bf16[384,1152]{1,0:T(8,128)(2,1)}, u32[]{:S(2)}, u32[]{:S(2)}) collective-permute-start(bf16[384,1152]{1,0:T(8,128)(2,1)} %constant_dynamic-slice_fusion.15), channel_id=1, source_target_pairs={{0,2},{2,0},{4,6},{6,4},{8,10},{10,8},{12,14},{14,12},{16,18},{18,... | collective-permute-start | bytes 2654216 | tf_op jit(solution)/shard_map/ppermute | solution.py:230
  261.5 49.8 %collective-permute-start.7 = (bf16[512,768]{1,0:T(8,128)(2,1)}, bf16[512,768]{1,0:T(8,128)(2,1)S(1)}, u32[]{:S(2)}, u32[]{:S(2)}) collective-permute-start(bf16[512,768]{1,0:T(8,128)(2,1)} %slice.166), channel_id=1, source_target_pairs={{0,1},{1,0},{2,3},{3,2},{4,5},{5,4},{6,7},{7,6},{8,9},{9,8},{10,11... | collective-permute-start | bytes 2359304 | tf_op jit(solution)/shard_map/ppermute | solution.py:227
  274.0 20.5 %collective-permute-start.36 = (bf16[48,1536]{1,0:T(8,128)(2,1)S(1)}, bf16[48,1536]{1,0:T(8,128)(2,1)S(1)}, u32[]{:S(2)}, u32[]{:S(2)}) collective-permute-start(bf16[48,1536]{1,0:T(8,128)(2,1)S(1)} %constant_dynamic-slice_fusion.4), channel_id=1, source_target_pairs={{0,16},{2,18},{4,20},{6,22},{8,24},{10,26},{12,28},{14,30},{16,0},... | collective-permute-start | bytes 442376 | tf_op jit(solution)/shard_map/ppermute | solution.py:230
  289.1 14.8 %collective-permute-start.44 = (bf16[96,768]{1,0:T(8,128)(2,1)S(1)}, bf16[96,768]{1,0:T(8,128)(2,1)S(1)}, u32[]{:S(2)}, u32[]{:S(2)}) collective-permute-start(bf16[96,768]{1,0:T(8,128)(2,1)S(1)} %constant_dynamic-slice_fusion), channel_id=1, source_target_pairs={{0,16},{2,18},{4,20},{6,22},{8,24},{10,26},{12,28},{14,30},{16,0},... | collective-permute-start | bytes 442376 | tf_op jit(solution)/shard_map/ppermute | solution.py:230
  311.2 19.2 %collective-permute-start.46 = (bf16[192,768]{1,0:T(8,128)(2,1)S(1)}, bf16[192,768]{1,0:T(8,128)(2,1)S(1)}, u32[]{:S(2)}, u32[]{:S(2)}) collective-permute-start(bf16[192,768]{1,0:T(8,128)(2,1)S(1)} %pad_maximum_fusion.15), channel_id=1, source_target_pairs={{0,8},{2,10},{4,12},{6,14},{8,0},{10,2},{12,4},{14,6},{16,24},{18,... | collective-permute-start | bytes 884744 | tf_op jit(solution)/shard_map/ppermute | solution.py:230
  313.5 24.2 %collective-permute-start.32 = (bf16[192,768]{1,0:T(8,128)(2,1)S(1)}, bf16[192,768]{1,0:T(8,128)(2,1)S(1)}, u32[]{:S(2)}, u32[]{:S(2)}) collective-permute-start(bf16[192,768]{1,0:T(8,128)(2,1)S(1)} %pad_maximum_fusion.13), channel_id=1, source_target_pairs={{0,2},{2,0},{4,6},{6,4},{8,10},{10,8},{12,14},{14,12},{16,18},{18,... | collective-permute-start | bytes 884744 | tf_op jit(solution)/shard_map/ppermute | solution.py:230
  317.5 38.2 %collective-permute-start.39 = (bf16[192,1536]{1,0:T(8,128)(2,1)S(1)}, bf16[192,1536]{1,0:T(8,128)(2,1)S(1)}, u32[]{:S(2)}, u32[]{:S(2)}) collective-permute-start(bf16[192,1536]{1,0:T(8,128)(2,1)S(1)} %pad_maximum_fusion.10), channel_id=1, source_target_pairs={{0,4},{2,6},{4,0},{6,2},{8,12},{10,14},{12,8},{14,10},{16,20},{18,... | collective-permute-start | bytes 1769480 | tf_op jit(solution)/shard_map/ppermute | solution.py:230
  330.5 22.6 %collective-permute-start.47 = (bf16[384,768]{1,0:T(8,128)(2,1)S(1)}, bf16[384,768]{1,0:T(8,128)(2,1)S(1)}, u32[]{:S(2)}, u32[]{:S(2)}) collective-permute-start(bf16[384,768]{1,0:T(8,128)(2,1)S(1)} %pad_maximum_fusion.11), channel_id=1, source_target_pairs={{0,4},{2,6},{4,0},{6,2},{8,12},{10,14},{12,8},{14,10},{16,20},{18,... | collective-permute-start | bytes 1769480 | tf_op jit(solution)/shard_map/ppermute | solution.py:230
  356.1 13.5 %collective-permute-start.40 = (bf16[384,1536]{1,0:T(8,128)(2,1)S(1)}, bf16[384,1536]{1,0:T(8,128)(2,1)S(1)}, u32[]{:S(2)}, u32[]{:S(2)}) collective-permute-start(bf16[384,1536]{1,0:T(8,128)(2,1)S(1)} %pad_maximum_fusion.3), channel_id=1, source_target_pairs={{0,2},{2,0},{4,6},{6,4},{8,10},{10,8},{12,14},{14,12},{16,18},{18,... | collective-permute-start | bytes 3538952 | tf_op jit(solution)/shard_map/ppermute | solution.py:230
  (66 other events, 1048.1 us)
